TPU v7x, 32 devices: a whole 2x2x4 slice. The times are simulated.
32 devices in a mesh: frame: 16 (over z, y, core), row: 2 (over x).
Axes of the slice: x: 2, y: 2, z: 4, core: 2. Of those that a mesh axis runs over, the one named last changes fastest.
Arguments:
- spatial_q: bfloat16 [16, 256, 3072], P('frame', 'row'), may hold values from -6 to 6
- spatial_k: bfloat16 [16, 256, 3072], P('frame', 'row'), may hold values from -6 to 6
- spatial_v: bfloat16 [16, 256, 3072], P('frame', 'row'), may hold values from -6 to 6
- norm_gain: float32 [3072], replicated, may hold values from 0.5 to 1.5
- temporal_weight: bfloat16 [3072, 3, 3072], P(None, None, 'row'), may hold values from -0.625 to 0.625
Outputs:
- temporal_out: bfloat16 [16, 256, 3072], P('frame', 'row')
All inputs are finite; a program needn't handle non-finite values.
Results may differ from a plain program's by a relative error of at most 0.0083.
Values may be sent and summed in bfloat16 or wider, within the bound.
No kernel may reach another device: no remote copies, remote signals or barrier semaphores. Data moves between devices by JAX's collectives and lax.ppermute only.
A program may use at most 64 MiB of HBM per device.

v0:
```python
import jax
import jax.numpy as jnp
from jax import lax
from jax.sharding import PartitionSpec as P

D = 3072
HEADS = 24
AGENTS = 128
epsilon = 1e-06


def local(spatial_q, spatial_k, spatial_v, norm_gain, temporal_weight):
    frame_count = lax.axis_size("frame")
    row_count = lax.axis_size("row")
    local_frames, local_tokens, width = spatial_q.shape
    head_size = D // HEADS
    scale = head_size ** (-0.5)
    pool_size = local_tokens * row_count // AGENTS
    own_agents = local_tokens // pool_size
    pooled = jnp.mean(
        spatial_q.reshape(local_frames, own_agents, pool_size, width), axis=2, dtype=jnp.float32
    )
    agents = lax.all_gather(pooled.astype(jnp.bfloat16), "row", axis=1, tiled=True)
    agent_heads = agents.reshape(local_frames, AGENTS, HEADS, head_size)
    query_heads = spatial_q.reshape(local_frames, local_tokens, HEADS, head_size)
    key_heads = spatial_k.reshape(local_frames, local_tokens, HEADS, head_size)
    value_heads = spatial_v.reshape(local_frames, local_tokens, HEADS, head_size)
    agent_scores = (
        jnp.einsum("fahd,fthd->fhat", agent_heads, key_heads, preferred_element_type=jnp.float32)
        * scale
    )
    peak = lax.pmax(jnp.max(agent_scores, axis=-1), "row")
    agent_weights = jnp.exp(agent_scores - peak[..., None])
    agent_totals = jnp.sum(agent_weights, axis=-1)
    agent_numer = jnp.einsum(
        "fhat,fthd->fhad",
        agent_weights.astype(jnp.bfloat16),
        value_heads,
        preferred_element_type=jnp.float32,
    )
    agent_totals, agent_numer = lax.psum((agent_totals, agent_numer), "row")
    agent_values = (agent_numer / agent_totals[..., None]).astype(jnp.bfloat16)
    token_scores = (
        jnp.einsum("fthd,fahd->fhta", query_heads, agent_heads, preferred_element_type=jnp.float32)
        * scale
    )
    token_weights = jax.nn.softmax(token_scores, axis=-1).astype(jnp.bfloat16)
    spatial_out = jnp.einsum(
        "fhta,fhad->fthd", token_weights, agent_values, preferred_element_type=jnp.float32
    )
    spatial_out = spatial_out.reshape(local_frames, local_tokens, width)
    mean_square = jnp.mean(spatial_out * spatial_out, axis=-1, keepdims=True)
    normed = (spatial_out * lax.rsqrt(mean_square + epsilon) * norm_gain).astype(jnp.bfloat16)
    slot_size = local_tokens // frame_count
    group_width = temporal_weight.shape[2]
    group_heads = group_width // head_size
    all_frames = local_frames * frame_count
    locations = row_count * slot_size
    packed = normed.reshape(local_frames, frame_count, slot_size, width)
    moved = lax.all_to_all(packed, "frame", split_axis=1, concat_axis=0, tiled=True)
    moved = moved.reshape(all_frames, slot_size, width)
    projected = jnp.einsum(
        "ftd,dcn->ftcn",
        lax.all_gather(moved, "row", axis=1, tiled=True),
        temporal_weight,
        preferred_element_type=jnp.float32,
    )
    qkv = projected.astype(jnp.bfloat16).reshape(all_frames, locations, 3, group_heads, head_size)
    temporal_scores = (
        jnp.einsum(
            "flhd,glhd->lhfg", qkv[:, :, 0], qkv[:, :, 1], preferred_element_type=jnp.float32
        )
        * scale
    )
    temporal_weights = jax.nn.softmax(temporal_scores, axis=-1).astype(jnp.bfloat16)
    attended = jnp.einsum(
        "lhfg,glhd->flhd", temporal_weights, qkv[:, :, 2], preferred_element_type=jnp.float32
    )
    attended = attended.astype(jnp.bfloat16).reshape(
        all_frames, row_count, 1, slot_size, group_width
    )
    gathered_heads = lax.all_to_all(attended, "row", split_axis=1, concat_axis=4, tiled=True)
    returned = lax.all_to_all(gathered_heads, "frame", split_axis=0, concat_axis=2, tiled=True)
    return returned.reshape(local_frames, local_tokens, width)


def solution(mesh):
    return jax.shard_map(
        local,
        mesh=mesh,
        in_specs=(
            P("frame", "row", None),
            P("frame", "row", None),
            P("frame", "row", None),
            P(),
            P(None, None, "row"),
        ),
        out_specs=P("frame", "row", None),
        check_vma=False,
    )
```

profile of v0, /device:TPU:1, one launch (start us, length us, event | category | flops | bytes accessed | tf_op | source)
XLA Modules:
  0.0 225.7 jit_solution(15268183589663754578)
XLA Ops:
  6.5 0.0 copy-start.3
  6.5 0.0 all-reduce.2.cloned.1.call-start
  6.5 0.0 copy-start
  6.5 2.3 %copy.102 = bf16[16,8,24,128]{3,2,1,0:T(8,128)(2,1)} copy(bf16[16,8,24,128]{3,1,2,0:T(8,128)(2,1)} %bitcast.101) | data formatting | bytes 1572864
  8.8 0.0 copy-done.3
  8.8 1.0 copy.103
  9.9 0.0 copy-done
  9.9 1.0 reshape.193
  10.8 1.9 reduce_sum.47
  12.8 11.5 %all-gather = bf16[128,3072]{1,0:T(8,128)(2,1)S(1)} all-gather(bf16[64,3072]{1,0:T(8,128)(2,1)S(1)} %multiply_convert_fusion), channel_id=2, replica_groups=mesh['frame'=16,'row'=2] {'row'}, dimensions={0}, use_global_device_ids=true | all-gather | bytes 1179648 | tf_op jit(solution)/shard_map/all_gather | solution.py:23
  24.3 0.4 copy.70
  24.7 1.5 fusion.45
  26.2 6.0 %pmax.7 = f32[24,128]{1,0:T(8,128)S(1)} all-reduce(f32[24,128]{1,0:T(8,128)S(1)} %get-tuple-element.8), channel_id=1, replica_groups=mesh['frame'=16,'row'=2] {'row'}, use_global_device_ids=true, to_apply=%region_2.0 | all-reduce | flops 3072 | bytes 24576 | tf_op jit(solution)/shard_map/pmax | solution.py:32
  32.2 2.8 %convolution_bitcast_fusion.1 = f32[1,24,128,128]{3,2,1,0:T(8,128)} fusion(f32[24,128,128]{1,2,0:T(8,128)S(1)} %get-tuple-element.9, bf16[128,24,128]{2,1,0:T(8,128)(2,1)} %bitcast.97, f32[24,128]{1,0:T(8,128)S(1)} %pmax.7), kind=kOutput, calls=%fused_computation.24 | convolution fusion | flops 101449728 | bytes 3944448 | tf_op jit(solution)/shard_map/fhat,fthd->fhad/dot_general | solution.py:35
  34.9 0.0 all-reduce.2.cloned.1.call-update
  35.0 0.0 all-gather.4.cloned.1.call-start
  35.0 1.0 copy.104
  36.0 0.0 copy-start.1
  36.1 0.3 fusion.17
  36.3 5.1 %psum.15 = f32[24,128]{1,0:T(8,128)S(1)} all-reduce(f32[24,128]{1,0:T(8,128)S(1)} %fusion.17), channel_id=1, replica_groups=mesh['frame'=16,'row'=2] {'row'}, use_global_device_ids=true, to_apply=%region_5.0 | all-reduce | flops 3072 | bytes 24576 | tf_op jit(solution)/shard_map/psum | solution.py:41
  41.5 0.0 copy-done.1
  41.5 1.1 fusion.42
  42.5 0.4 convolution_multiply_fusion
  42.9 46.9 %all-reduce.2.cloned.1.call-done = f32[1,24,128,128]{3,2,1,0:T(8,128)} async-done(((f32[1,24,128,128]{3,2,1,0:T(8,128)}), f32[1,24,128,128]{3,2,1,0:T(8,128)}) %all-reduce.2.cloned.1.call-update) | async-done | bytes 1572880 | tf_op jit(solution)/shard_map/psum | solution.py:41
  89.8 9.1 %multiply_reduce_fusion = (f32[128]{0:T(128)S(1)}, f32[1,128,24,128]{1,3,2,0:T(8,128)}) fusion(f32[24,128]{1,0:T(8,128)S(1)} %fusion.42, f32[24,128,128]{1,2,0:T(8,128)S(1)} %convolution_multiply_fusion, f32[1,24,128,128]{3,2,1,0:T(8,128)} %all-reduce.2.cloned.1.call-done, f32[24,128]{1,0:T(8,128)S(1)} %psum.15), kind=kOutput, calls=%fused_computation.14 | convolution fusion | flops 103418880 | bytes 4743680 | tf_op jit(solution)/shard_map/fhta,fhad->fthd/dot_general | solution.py:48
  98.9 0.1 rsqrt.12
  98.9 0.0 copy-start.4
  98.9 2.0 copy.79
  100.9 0.0 copy-done.4
  100.9 0.4 fusion.21
  101.3 26.9 %all_to_all.36 = bf16[1,16,8,3072]{3,2,0,1:T(8,128)(2,1)} all-to-all(bf16[1,16,8,3072]{3,2,0,1:T(8,128)(2,1)S(1)} %fusion.21), channel_id=1, replica_groups=mesh['frame'=16,'row'=2] {'frame'}, dimensions={1} | all-to-all | bytes 1572864 | tf_op jit(solution)/shard_map/all_to_all | solution.py:60
  128.2 0.0 all-gather.4.cloned.1.call-update
  128.3 24.4 %all-gather.4.cloned.1.call-done = bf16[1,16,16,3072]{3,2,1,0:T(8,128)(2,1)} async-done(((bf16[1,16,8,3072]{3,2,1,0:T(8,128)(2,1)}), bf16[1,16,16,3072]{3,2,1,0:T(8,128)(2,1)}) %all-gather.4.cloned.1.call-update) | async-done | bytes 1572880 | tf_op jit(solution)/shard_map/all_gather | solution.py:64
  152.7 14.4 %fusion.4 = bf16[16,16,3,1536]{3,1,2,0:T(8,128)(2,1)} fusion(bf16[3072,3,1536]{2,0,1:T(8,128)(2,1)} %param.9, bf16[1,16,16,3072]{3,2,1,0:T(8,128)(2,1)} %all-gather.4.cloned.1.call-done), kind=kOutput, calls=%fused_computation.4 | convolution fusion | flops 7248936960 | bytes 32243712 | tf_op jit(solution)/shard_map/ftd,dcn->ftcn/dot_general | solution.py:62
  167.1 4.2 %reshape.188 = bf16[16,16,3,12,128]{4,3,1,2,0:T(8,128)(2,1)S(1)} reshape(bf16[16,16,3,1536]{3,1,2,0:T(8,128)(2,1)} %fusion.4) | data formatting | bytes 4718592 | tf_op jit(solution)/shard_map/reshape | solution.py:68
  171.3 1.9 fusion.41
  173.1 0.0 copy-start.2
  173.1 3.1 %fusion.48 = (f32[16,12,16]{2,1,0:T(8,128)S(1)}, f32[16,12,16,16]{2,3,1,0:T(8,128)S(1)}) fusion(bf16[16,16,1,12,128]{4,3,1,2,0:T(8,128)(2,1)} %get-tuple-element.7, bf16[16,16,1,12,128]{4,3,1,2,0:T(8,128)(2,1)} %get-tuple-element.6), kind=kOutput, calls=%fused_computation.49 | convolution fusion | flops 12730383 | bytes 1781760 | tf_op jit(solution)/shard_map/sub | solution.py:75
  176.2 0.0 copy-done.2
  176.2 0.7 fusion.19
  176.9 0.3 copy.87
  177.2 0.5 reshape.189
  177.7 0.1 copy.88
  177.8 12.5 %all_to_all.37 = bf16[16,2,1,8,1536]{4,3,0,2,1:T(8,128)(2,1)S(1)} all-to-all(bf16[16,2,1,8,1536]{4,3,0,2,1:T(8,128)(2,1)S(1)} %copy.88), channel_id=1, replica_groups=mesh['frame'=16,'row'=2] {'row'}, dimensions={1} | all-to-all | bytes 1572864 | tf_op jit(solution)/shard_map/all_to_all | solution.py:82
  190.3 0.1 copy.101
  190.4 27.6 %all_to_all.38 = bf16[16,1,1,8,3072]{4,3,2,1,0:T(8,128)(2,1)S(1)} all-to-all(bf16[16,1,1,8,3072]{4,3,2,1,0:T(8,128)(2,1)S(1)} %bitcast.94), channel_id=1, replica_groups=mesh['frame'=16,'row'=2] {'frame'}, dimensions={0} | all-to-all | bytes 1572864 | tf_op jit(solution)/shard_map/all_to_all | solution.py:83
  218.0 0.9 copy.146
  (2 shorter events, 0.1 us)
Async XLA Ops:
  6.5 2.3 %copy-start.3 = (bf16[1,128,3072]{2,1,0:T(8,128)(2,1)S(1)}, bf16[1,128,3072]{2,1,0:T(8,128)(2,1)}, u32[]{:S(2)}) copy-start(bf16[1,128,3072]{2,1,0:T(8,128)(2,1)} %param.7) | copy-start | bytes 2359300
  6.5 83.2 %all-reduce.2.cloned.1.call-start = ((), (), s32[]{:S(2)}) async-start(), calls=%async_computation.3 | async-start | bytes 3145728 | tf_op jit(solution)/shard_map/psum | solution.py:41
  6.5 3.3 %copy-start = (bf16[1,128,3072]{2,1,0:T(8,128)(2,1)S(1)}, bf16[1,128,3072]{2,1,0:T(8,128)(2,1)}, u32[]{:S(2)}) copy-start(bf16[1,128,3072]{2,1,0:T(8,128)(2,1)} %param.5) | copy-start | bytes 2359300
  35.0 117.7 %all-gather.4.cloned.1.call-start = ((), (), s32[]{:S(2)}) async-start(), calls=%async_computation.4 | async-start | bytes 2359296 | tf_op jit(solution)/shard_map/all_gather | solution.py:64
  36.0 5.4 %copy-start.1 = (bf16[16,8,24,128]{3,2,1,0:T(8,128)(2,1)S(1)}, bf16[16,8,24,128]{3,2,1,0:T(8,128)(2,1)}, u32[]{:S(2)}) copy-start(bf16[16,8,24,128]{3,2,1,0:T(8,128)(2,1)} %copy.104) | copy-start | bytes 2359300
  98.9 2.0 copy-start.4
  173.1 3.1 %copy-start.2 = (bf16[16,16,1,12,128]{4,3,1,2,0:T(8,128)(2,1)S(1)}, bf16[16,16,1,12,128]{4,3,1,2,0:T(8,128)(2,1)}, u32[]{:S(2)}) copy-start(bf16[16,16,1,12,128]{4,3,1,2,0:T(8,128)(2,1)} %get-tuple-element.5) | copy-start | bytes 2359300
Sparse Core Ops, SparseCore 0:
  35.1 54.6 all-reduce.1
  128.4 24.2 all-gather.3
where the time goes:
time: 226 us
  blocking collectives  89.7 us (40%)
  waiting for transfers between devices  71.3 us (32%)
  matrix products  32.9 us (15%)
  local copies, waits for them, and re-layouts  15.6 us (7%)
  between operations  13.5 us (6%)
  other arithmetic  2.59 us (1%)
    psum x1, waiting for transfers between devices, local(): agent_totals, agent_numer = lax.psum((agent_totals, agent_numer), 'row')  46.9 us
    all_to_all x1, blocking collectives, local(): lax.all_to_all(gathered_heads, 'frame', split_axis=0, concat_axis=2, tile...  27.6 us
    all_to_all x1, blocking collectives, local(): lax.all_to_all(packed, 'frame', split_axis=1, concat_axis=0, tiled=True)  26.9 us
    all_gather x1, waiting for transfers between devices, local(): lax.all_gather(moved, 'row', axis=1, tiled=True)  24.4 us
    dot_general x1, matrix products, local(): jnp.einsum('ftd,dcn->ftcn', lax.all_gather(moved, 'row', axis=1, tiled=Tr...  14.4 us
    all_to_all x1, blocking collectives, local(): lax.all_to_all(attended, 'row', split_axis=1, concat_axis=4, tiled=True)  12.5 us
    all_gather x1, blocking collectives, local(): lax.all_gather(pooled.astype(jnp.bfloat16), 'row', axis=1, tiled=True)  11.5 us
    dot_general x1, matrix products, local(): jnp.einsum('fhta,fhad->fthd', token_weights, agent_values, preferred_elem...  9.07 us
  transfers between devices with their start and end apart: 2, of which 2 were waited for; matrix products, arithmetic and copies ran while one was open for 1% of the time, Pallas kernels for 0%

commit v1 on v0

--- a/solution.py
+++ b/solution.py
@@ -59,12 +59,21 @@
     packed = normed.reshape(local_frames, frame_count, slot_size, width)
     moved = lax.all_to_all(packed, "frame", split_axis=1, concat_axis=0, tiled=True)
     moved = moved.reshape(all_frames, slot_size, width)
-    projected = jnp.einsum(
-        "ftd,dcn->ftcn",
-        lax.all_gather(moved, "row", axis=1, tiled=True),
-        temporal_weight,
-        preferred_element_type=jnp.float32,
-    )
+    size, here, extent = (lax.axis_size("row"), lax.axis_index("row"), moved.shape[1])
+    forward = [(i, (i + 1) % size) for i in range(size)]
+    current, out = (moved, None)
+    for hop in range(size):
+        source = (here - hop) % size
+        upcoming = lax.ppermute(current, "row", forward) if hop < size - 1 else None
+        made = jnp.einsum(
+            "ftd,dcn->ftcn", current, temporal_weight, preferred_element_type=jnp.float32
+        )
+        length = made.shape[1]
+        if out is None:
+            out = jnp.zeros((*made.shape[:1], size * length, *made.shape[1 + 1 :]), made.dtype)
+        out = lax.dynamic_update_slice_in_dim(out, made, source * length, axis=1)
+        current = upcoming
+    projected = out
     qkv = projected.astype(jnp.bfloat16).reshape(all_frames, locations, 3, group_heads, head_size)
     temporal_scores = (
         jnp.einsum(

time: 226 us -> 213 us (0.942)
  blocking collectives: 89.7 us -> 62.8 us
  matrix products: 32.9 us -> 43.1 us
  starting transfers between devices: 0.04 us -> 6.65 us
  waiting for transfers between devices: 71.3 us -> 67.4 us
    all_to_all x1 -> x0, blocking collectives: 26.9 us -> none  [local(): lax.all_to_all(packed, 'frame', split_axis=1, concat_axis=0, tiled=True)]
    all_gather x1 -> x0, waiting for transfers between devices: 24.4 us -> none  [local(): lax.all_gather(moved, 'row', axis=1, tiled=True)]
    all_to_all x0 -> x1, waiting for transfers between devices: none -> 18.6 us  [local(): lax.all_to_all(packed, 'frame', split_axis=1, concat_axis=0, tiled=True)]
    dot_general x1 -> x2, matrix products: 14.4 us -> 28 us  [local(): jnp.einsum('ftd,dcn->ftcn', current, temporal_weight, preferred_element_t...]
    all_to_all x0 -> x1, starting transfers between devices: none -> 6.37 us  [local(): lax.all_to_all(packed, 'frame', split_axis=1, concat_axis=0, tiled=True)]
    ppermute x0 -> x1, waiting for transfers between devices: none -> 3 us  [local(): upcoming = lax.ppermute(current, 'row', forward) if hop < size - 1 else None]
    unnamed x14 -> x16, local copies, waits for them, and re-layouts: 5.24 us -> 3.4 us
  transfers between devices with their start and end apart: 2 -> 3, of which waited for: 2 -> 3; matrix products, arithmetic and copies ran while one was open for 1% -> 9% of each run, Pallas kernels for 0% -> 0%
where the time goes in v1:
time: 213 us; the launch traced here: 212 us
  waiting for transfers between devices  67.4 us (32%)
  blocking collectives  62.8 us (29%)
  matrix products  43.1 us (20%)
  local copies, waits for them, and re-layouts  15.4 us (7%)
  between operations  13.6 us (6%)
  starting transfers between devices  6.65 us (3%)
  other arithmetic  3.46 us (2%)
    psum x1, waiting for transfers between devices, local(): agent_totals, agent_numer = lax.psum((agent_totals, agent_numer), 'row')  45.8 us
    dot_general x2, matrix products, local(): jnp.einsum('ftd,dcn->ftcn', current, temporal_weight, preferred_element_t...  28 us
    all_to_all x1, blocking collectives, local(): lax.all_to_all(gathered_heads, 'frame', split_axis=0, concat_axis=2, tile...  27.7 us
    all_to_all x1, waiting for transfers between devices, local(): lax.all_to_all(packed, 'frame', split_axis=1, concat_axis=0, tiled=True)  18.6 us
    all_to_all x1, blocking collectives, local(): lax.all_to_all(attended, 'row', split_axis=1, concat_axis=4, tiled=True)  12.3 us
    all_gather x1, blocking collectives, local(): lax.all_gather(pooled.astype(jnp.bfloat16), 'row', axis=1, tiled=True)  11.7 us
    dot_general x1, matrix products, local(): jnp.einsum('fhta,fhad->fthd', token_weights, agent_values, preferred_elem...  7.95 us
    all_to_all x1, starting transfers between devices, local(): lax.all_to_all(packed, 'frame', split_axis=1, concat_axis=0, tiled=True)  6.37 us
  transfers between devices with their start and end apart: 3, of which 3 were waited for; matrix products, arithmetic and copies ran while one was open for 9% of the time, Pallas kernels for 0%

profile of v1, /device:TPU:1, one launch (start us, length us, event | category | flops | bytes accessed | tf_op | source)
XLA Modules:
  0.0 212.4 jit_solution(316546721894746054)
XLA Ops:
  6.5 0.0 all-reduce.2.cloned.1.call-start
  6.5 2.2 %reshape.193 = f32[64,2,3072]{2,1,0:T(2,128)S(1)} reshape(bf16[1,128,3072]{2,1,0:T(8,128)(2,1)} %param.5) | data formatting | bytes 2359296 | tf_op jit(solution)/shard_map/convert_element_type | solution.py:20
  8.7 1.9 reduce_sum.47
  10.6 0.0 copy-start.3
  10.6 11.7 %all-gather = bf16[128,3072]{1,0:T(8,128)(2,1)S(1)} all-gather(bf16[64,3072]{1,0:T(8,128)(2,1)S(1)} %multiply_convert_fusion), channel_id=2, replica_groups=mesh['frame'=16,'row'=2] {'row'}, dimensions={0}, use_global_device_ids=true | all-gather | bytes 1179648 | tf_op jit(solution)/shard_map/all_gather | solution.py:23
  22.3 0.4 copy.65
  22.7 0.0 copy-done.3
  22.7 0.2 copy.97
  22.8 0.0 copy-start.4
  22.9 0.4 fusion.51
  23.2 6.0 %pmax.7 = f32[24,128]{1,0:T(8,128)S(1)} all-reduce(f32[24,128]{1,0:T(8,128)S(1)} %get-tuple-element.8), channel_id=1, replica_groups=mesh['frame'=16,'row'=2] {'row'}, use_global_device_ids=true, to_apply=%region_2.0 | all-reduce | flops 3072 | bytes 24576 | tf_op jit(solution)/shard_map/pmax | solution.py:32
  29.2 0.0 copy-done.4
  29.2 0.2 copy.98
  29.4 1.6 convolution_bitcast_fusion.1
  31.0 0.0 copy-start
  31.0 0.0 all-reduce.2.cloned.1.call-update
  31.1 1.1 copy-done
  32.2 1.0 copy.99
  33.2 0.3 fusion.21
  33.5 5.1 %psum.15 = f32[24,128]{1,0:T(8,128)S(1)} all-reduce(f32[24,128]{1,0:T(8,128)S(1)} %fusion.21), channel_id=1, replica_groups=mesh['frame'=16,'row'=2] {'row'}, use_global_device_ids=true, to_apply=%region_5.0 | all-reduce | flops 3072 | bytes 24576 | tf_op jit(solution)/shard_map/psum | solution.py:41
  38.6 0.0 copy-done.1
  38.6 1.1 fusion.48
  39.7 0.4 convolution_multiply_fusion
  40.1 45.8 %all-reduce.2.cloned.1.call-done = f32[1,24,128,128]{3,2,1,0:T(8,128)} async-done(((f32[1,24,128,128]{3,2,1,0:T(8,128)}), f32[1,24,128,128]{3,2,1,0:T(8,128)}) %all-reduce.2.cloned.1.call-update) | async-done | bytes 1572880 | tf_op jit(solution)/shard_map/psum | solution.py:41
  85.9 7.9 %multiply_reduce_fusion = (f32[128]{0:T(128)S(1)}, f32[1,128,24,128]{1,3,2,0:T(8,128)S(1)}) fusion(f32[24,128]{1,0:T(8,128)S(1)} %fusion.48, f32[24,128,128]{1,2,0:T(8,128)S(1)} %convolution_multiply_fusion, f32[1,24,128,128]{3,2,1,0:T(8,128)} %all-reduce.2.cloned.1.call-done, f32[24,128]{1,0:T(8,128)S(1)} %psum.15), kind=kOutput, calls=%fused_computation.16 | convolution fusion | flops 103418880 | bytes 4743680 | tf_op jit(solution)/shard_map/fhta,fhad->fthd/dot_general | solution.py:48
  93.8 0.6 copy.74
  94.4 0.1 rsqrt.12
  94.5 0.0 copy-done.5
  94.5 1.3 fusion.25
  95.8 6.4 %all-to-all-start = ((bf16[1,16,8,3072]{3,2,0,1:T(8,128)(2,1)}), bf16[1,16,8,3072]{3,2,0,1:T(8,128)(2,1)S(1)}, u32[]{:S(2)}, u32[]{:S(2)}) async-start(bf16[1,16,8,3072]{3,2,0,1:T(8,128)(2,1)} %fusion.25), calls=%async_computation | async-start | bytes 1572864 | tf_op jit(solution)/shard_map/all_to_all | solution.py:60
  102.2 18.6 %all-to-all-done = bf16[1,16,8,3072]{3,2,0,1:T(8,128)(2,1)S(1)} async-done(((bf16[1,16,8,3072]{3,2,0,1:T(8,128)(2,1)}), bf16[1,16,8,3072]{3,2,0,1:T(8,128)(2,1)S(1)}, u32[]{:S(2)}, u32[]{:S(2)}) %all-to-all-start) | async-done | bytes 786464 | tf_op jit(solution)/shard_map/all_to_all | solution.py:60
  120.8 0.3 collective-permute-start
  121.1 1.7 broadcast_in_dim.2
  122.8 14.0 %fusion.6 = bf16[16,16,3,1536]{3,1,2,0:T(8,128)(2,1)} fusion(bf16[16,16,3,1536]{3,1,2,0:T(8,128)(2,1)} %broadcast_in_dim.2, s32[]{:T(128)S(6)} %select_n.18, bf16[3072,3,1536]{2,0,1:T(8,128)(2,1)} %param.9, bf16[1,16,8,3072]{3,2,0,1:T(8,128)(2,1)S(1)} %all-to-all-done), kind=kOutput, calls=%fused_computation.6 | convolution fusion | flops 3623878656 | bytes 31457284 | tf_op jit(solution)/shard_map/ftd,dcn->ftcn/dot_general | solution.py:68
  136.7 3.0 %collective-permute-done = bf16[16,8,3072]{2,1,0:T(8,128)(2,1)S(1)} collective-permute-done((bf16[16,8,3072]{2,1,0:T(8,128)(2,1)S(1)}, bf16[16,8,3072]{2,1,0:T(8,128)(2,1)S(1)}, u32[]{:S(2)}, u32[]{:S(2)}) %collective-permute-start) | collective-permute-done | bytes 786464 | tf_op jit(solution)/shard_map/ppermute | solution.py:67
  139.7 14.0 %fusion.9 = bf16[16,16,3,1536]{3,1,2,0:T(8,128)(2,1)} fusion(bf16[16,16,3,1536]{3,1,2,0:T(8,128)(2,1)} %fusion.6, s32[]{:T(128)S(6)} %select_n.20, bf16[3072,3,1536]{2,0,1:T(8,128)(2,1)} %param.9, bf16[16,8,3072]{2,1,0:T(8,128)(2,1)S(1)} %collective-permute-done), kind=kOutput, calls=%fused_computation.7 | convolution fusion | flops 3623878656 | bytes 31457284 | tf_op jit(solution)/shard_map/ftd,dcn->ftcn/dot_general | solution.py:68
  153.7 4.4 %reshape.188 = bf16[16,16,3,12,128]{4,3,1,2,0:T(8,128)(2,1)S(1)} reshape(bf16[16,16,3,1536]{3,1,2,0:T(8,128)(2,1)} %fusion.9) | data formatting | bytes 4718592 | tf_op jit(solution)/shard_map/reshape | solution.py:77
  158.1 1.9 fusion.47
  160.0 3.1 %fusion.54 = (f32[16,12,16]{2,1,0:T(8,128)S(1)}, f32[16,12,16,16]{2,3,1,0:T(8,128)S(1)}) fusion(bf16[16,16,1,12,128]{4,3,1,2,0:T(8,128)(2,1)} %get-tuple-element.7, bf16[16,16,1,12,128]{4,3,1,2,0:T(8,128)(2,1)} %get-tuple-element.6), kind=kOutput, calls=%fused_computation.53 | convolution fusion | flops 12730383 | bytes 1781760 | tf_op jit(solution)/shard_map/sub | solution.py:84
  163.1 0.0 copy-done.2
  163.1 0.7 fusion.23
  163.8 0.3 copy.81
  164.1 0.5 reshape.189
  164.6 0.1 copy.82
  164.6 12.3 %all_to_all.36 = bf16[16,2,1,8,1536]{4,3,0,2,1:T(8,128)(2,1)S(1)} all-to-all(bf16[16,2,1,8,1536]{4,3,0,2,1:T(8,128)(2,1)S(1)} %copy.82), channel_id=1, replica_groups=mesh['frame'=16,'row'=2] {'row'}, dimensions={1} | all-to-all | bytes 1572864 | tf_op jit(solution)/shard_map/all_to_all | solution.py:91
  176.9 0.1 copy.96
  177.0 27.7 %all_to_all.37 = bf16[16,1,1,8,3072]{4,3,2,1,0:T(8,128)(2,1)S(1)} all-to-all(bf16[16,1,1,8,3072]{4,3,2,1,0:T(8,128)(2,1)S(1)} %bitcast.102), channel_id=1, replica_groups=mesh['frame'=16,'row'=2] {'frame'}, dimensions={0} | all-to-all | bytes 1572864 | tf_op jit(solution)/shard_map/all_to_all | solution.py:92
  204.7 0.9 copy.143
  (5 shorter events, 0.1 us)
Async XLA Ops:
  6.5 79.3 %all-reduce.2.cloned.1.call-start = ((), (), s32[]{:S(2)}) async-start(), calls=%async_computation.3 | async-start | bytes 3145728 | tf_op jit(solution)/shard_map/psum | solution.py:41
  10.6 12.0 %copy-start.3 = (bf16[1,128,3072]{2,1,0:T(8,128)(2,1)S(1)}, bf16[1,128,3072]{2,1,0:T(8,128)(2,1)}, u32[]{:S(2)}) copy-start(bf16[1,128,3072]{2,1,0:T(8,128)(2,1)} %param.6) | copy-start | bytes 2359300
  22.8 6.4 %copy-start.4 = (bf16[1,128,3072]{2,1,0:T(8,128)(2,1)S(1)}, bf16[1,128,3072]{2,1,0:T(8,128)(2,1)}, u32[]{:S(2)}) copy-start(bf16[1,128,3072]{2,1,0:T(8,128)(2,1)} %param.7) | copy-start | bytes 2359300
  31.0 1.1 copy-start
  33.2 5.4 %copy-start.1 = (bf16[16,8,24,128]{3,2,1,0:T(8,128)(2,1)S(1)}, bf16[16,8,24,128]{3,2,1,0:T(8,128)(2,1)}, u32[]{:S(2)}) copy-start(bf16[16,8,24,128]{3,2,1,0:T(8,128)(2,1)} %copy.99) | copy-start | bytes 2359300
  93.8 0.7 copy-start.5
  95.8 25.0 %all-to-all-start = ((bf16[1,16,8,3072]{3,2,0,1:T(8,128)(2,1)}), bf16[1,16,8,3072]{3,2,0,1:T(8,128)(2,1)S(1)}, u32[]{:S(2)}, u32[]{:S(2)}) async-start(bf16[1,16,8,3072]{3,2,0,1:T(8,128)(2,1)} %fusion.25), calls=%async_computation | async-start | bytes 1572864 | tf_op jit(solution)/shard_map/all_to_all | solution.py:60
  120.8 18.9 %collective-permute-start = (bf16[16,8,3072]{2,1,0:T(8,128)(2,1)S(1)}, bf16[16,8,3072]{2,1,0:T(8,128)(2,1)S(1)}, u32[]{:S(2)}, u32[]{:S(2)}) collective-permute-start(bf16[16,8,3072]{2,1,0:T(8,128)(2,1)S(1)} %bitcast.100), channel_id=1, source_target_pairs={{0,1},{1,0},{2,3},{3,2},{4,5},{5,4},{6,7},{7,6},{8,9},{9,8},{10,11... | collective-permute-start | bytes 2359304 | tf_op jit(solution)/shard_map/ppermute | solution.py:67
  160.0 3.1 %copy-start.2 = (bf16[16,16,1,12,128]{4,3,1,2,0:T(8,128)(2,1)S(1)}, bf16[16,16,1,12,128]{4,3,1,2,0:T(8,128)(2,1)}, u32[]{:S(2)}) copy-start(bf16[16,16,1,12,128]{4,3,1,2,0:T(8,128)(2,1)} %get-tuple-element.5) | copy-start | bytes 2359300
Sparse Core Ops, SparseCore 0:
  31.2 54.6 all-reduce.1
